TPU v7x, 32 devices: a whole 2x2x4 slice. The times are simulated.
32 devices in a mesh: lon: 8 (over y, x, core), lat: 4 (over z).
Axes of the slice: x: 2, y: 2, z: 4, core: 2. Of those that a mesh axis runs over, the one named last changes fastest.
Arguments:
- fields: float32 [5, 1, 128, 11520], P(None, None, 'lat', 'lon'), may hold values from -6 to 6
- frac_x: float32 [2, 1, 128], replicated, may hold values from 0.05 to 0.95
- frac_y: float32 [2, 1, 128], replicated, may hold values from 0.05 to 0.9
- shift_cells: int32 [2, 1, 128], replicated, may hold values from -5760 to 5759, as said below
- polar_mask: int32 [128], replicated, may hold values from 0 to 1, as said below
Outputs:
- fields_out: float32 [5, 1, 128, 11520], P(None, None, 'lat', 'lon')
Inputs may be any that keep to these rules, and one draw needn't show every extreme that they name: `shift_cells`: outside the first and last 32 rows every count lies in -2 .. 1, and both -2 and 1 occur there. `polar_mask`: nonzero only in the first and last 32 rows; the first and the last row are 1.
All inputs are finite; a program needn't handle non-finite values.
Results may differ from a plain program's by a relative error of at most 0.00016.
Values sent between devices are 32-bit elements; how exact they have to be, the bound alone decides.
A program may use at most 64 MiB of HBM per device.

v0:
```python
import math
import jax
import jax.numpy as jnp
from jax import lax
from jax.sharding import PartitionSpec as P

FA = 90
FB = 128
SUBS = 2
REACH = 4


def passed_along(x, axis, by):
    devices = lax.axis_size(axis)
    return lax.ppermute(x, axis, [(i, (i + by) % devices) for i in range(devices)])


def passed_along_2(block, axis, distance):
    devices = range(lax.axis_size(axis))
    route = [(i - distance, i) for i in devices if i - distance in devices]
    return lax.ppermute(block, axis, route)


def roll_digits(values, amount, span, axis):
    bit_total = max((span - 1).bit_length(), 1)
    for bit in range(bit_total):
        moved = jnp.roll(values, 1 << bit, axis=axis)
        taken = amount >> bit & 1 == 1
        values = jnp.where(taken, moved, values)
    return values


def cycle_move(state, counts, lon_cells):
    device_jump = jnp.floor_divide(counts, lon_cells)
    remainder = counts - device_jump * lon_cells
    select = device_jump + REACH
    bit_count = (2 * REACH).bit_length() - 1
    offsets = [-REACH] + [1 << bit for bit in range(bit_count)]
    current = state
    for turn, offset in enumerate(offsets):
        moved = passed_along(current, "lon", offset)
        if turn == 0:
            current = moved
        else:
            taken = select >> turn - 1 & 1 == 1
            current = jnp.where(taken[None, :, :, None], moved, current)
    western = passed_along(current, "lon", 1)
    joined = jnp.concatenate([western, current], axis=3)
    rolled = roll_digits(joined, remainder[None, :, :, None], lon_cells, 3)
    return rolled[:, :, :, lon_cells:]


def zonal_fraction(whole, courant):
    previous = jnp.roll(whole, 1, axis=1)
    edge = whole + 0.5 * (1.0 - courant) * (whole - previous)
    return whole - courant * (edge - jnp.roll(edge, 1, axis=1))


def polar_smooth(whole, lat_rows, marks, lat_cells, lat_total):
    row_count, lon_total = whole.shape
    highest = lax.Precision.HIGHEST
    first_ids = jnp.arange(FA, dtype=jnp.int32)
    second_ids = jnp.arange(FB, dtype=jnp.int32)
    angle_first = (
        2.0 * math.pi * (first_ids[:, None] * first_ids[None, :] % FA).astype(jnp.float32) / FA
    )
    cos_first, sin_first = (jnp.cos(angle_first), jnp.sin(angle_first))
    angle_second = (
        2.0 * math.pi * (second_ids[:, None] * second_ids[None, :] % FB).astype(jnp.float32) / FB
    )
    cos_second, sin_second = (jnp.cos(angle_second), jnp.sin(angle_second))
    angle_twist = (
        2.0
        * math.pi
        * (first_ids[:, None] * second_ids[None, :] % lon_total).astype(jnp.float32)
        / lon_total
    )
    cos_twist, sin_twist = (jnp.cos(angle_twist), jnp.sin(angle_twist))
    waves = (first_ids[:, None] + FA * second_ids[None, :]).astype(jnp.float32)
    sine = jnp.sin(math.pi * waves / lon_total)
    phi = math.pi * (lat_rows.astype(jnp.float32) + 0.5) / lat_total - math.pi / 2
    edge_cos = math.sin(math.pi * (lat_cells - 0.5) / lat_total)
    b_val = jnp.cos(phi) / edge_cos
    gain = 1.0 / (1.0 + sine[None, :, :] ** 2 / b_val[:, None, None] ** 2)
    grid = whole.reshape(row_count, FA, FB)
    real_one = jnp.einsum("kn,rnm->rkm", cos_first, grid, precision=highest)
    imag_one = -jnp.einsum("kn,rnm->rkm", sin_first, grid, precision=highest)
    real_two = real_one * cos_twist + imag_one * sin_twist
    imag_two = imag_one * cos_twist - real_one * sin_twist
    real_spec = jnp.einsum("rkm,mq->rkq", real_two, cos_second, precision=highest) + jnp.einsum(
        "rkm,mq->rkq", imag_two, sin_second, precision=highest
    )
    imag_spec = jnp.einsum("rkm,mq->rkq", imag_two, cos_second, precision=highest) - jnp.einsum(
        "rkm,mq->rkq", real_two, sin_second, precision=highest
    )
    real_spec = real_spec * gain
    imag_spec = imag_spec * gain
    real_back = jnp.einsum("rkq,mq->rkm", real_spec, cos_second, precision=highest) - jnp.einsum(
        "rkq,mq->rkm", imag_spec, sin_second, precision=highest
    )
    imag_back = jnp.einsum("rkq,mq->rkm", imag_spec, cos_second, precision=highest) + jnp.einsum(
        "rkq,mq->rkm", real_spec, sin_second, precision=highest
    )
    real_turn = real_back * cos_twist - imag_back * sin_twist
    imag_turn = imag_back * cos_twist + real_back * sin_twist
    result = jnp.einsum("kn,rkm->rnm", cos_first, real_turn, precision=highest) - jnp.einsum(
        "kn,rkm->rnm", sin_first, imag_turn, precision=highest
    )
    result = result.reshape(row_count, lon_total) / lon_total
    return jnp.where((marks == 1)[:, None], result, whole)


def meridional(state, merid_step, first_row):
    n_fields, n_levels, lat_cells, lon_cells = state.shape
    southern = passed_along_2(state[:, :, lat_cells - 2 :, :], "lat", 1)
    extended = jnp.concatenate([southern, state], axis=2)
    padded_faces = jnp.concatenate([merid_step, jnp.zeros((n_levels, 1), jnp.float32)], axis=1)
    faces = lax.dynamic_slice_in_dim(padded_faces, first_row, lat_cells + 1, 1)
    face_ids = first_row + jnp.arange(lat_cells + 1, dtype=jnp.int32)
    faces = jnp.where((face_ids == 0)[None, :], jnp.zeros_like(faces), faces)
    courant = faces[None, :, :, None]
    upper = extended[:, :, 1 : lat_cells + 2, :]
    lower = extended[:, :, 0 : lat_cells + 1, :]
    flux = courant * (upper + 0.5 * (1.0 - courant) * (upper - lower))
    return state + flux[:, :, :lat_cells, :] - flux[:, :, 1:, :]


def body(fields, frac_x, frac_y, shift_cells, polar_mask):
    n_fields, n_levels, lat_cells, lon_cells = fields.shape
    lon_devs = lax.axis_size("lon")
    lat_total = lat_cells * lax.axis_size("lat")
    lon_index = lax.axis_index("lon")
    first_row = lax.axis_index("lat") * lat_cells
    row_total = n_fields * n_levels * lat_cells
    per_device = row_total // lon_devs
    row_start = lon_index * per_device
    local_rows = first_row + jnp.arange(lat_cells, dtype=jnp.int32)
    marks_local = lax.dynamic_slice_in_dim(polar_mask, first_row, lat_cells, 0)

    def my_rows(table):
        spread = jnp.broadcast_to(table[None], (n_fields, n_levels, lat_cells)).reshape(row_total)
        return lax.dynamic_slice_in_dim(spread, row_start, per_device, 0)

    row_lats = my_rows(local_rows[None])
    row_marks = my_rows(marks_local[None])
    state = fields
    for substep in range(SUBS):
        counts = lax.dynamic_slice_in_dim(shift_cells[substep], first_row, lat_cells, 1)
        fractions = lax.dynamic_slice_in_dim(frac_x[substep], first_row, lat_cells, 1)
        placed = cycle_move(state, counts, lon_cells)
        flat = placed.reshape(row_total, lon_cells)
        whole = lax.all_to_all(flat, "lon", split_axis=0, concat_axis=1, tiled=True)
        whole = zonal_fraction(whole, my_rows(fractions)[:, None])
        whole = polar_smooth(whole, row_lats, row_marks, lat_cells, lat_total)
        blocks = lax.all_to_all(whole, "lon", split_axis=1, concat_axis=0, tiled=True)
        state = blocks.reshape(n_fields, n_levels, lat_cells, lon_cells)
        state = meridional(state, frac_y[substep], first_row)
    return state


def solution(mesh):
    return jax.shard_map(
        body,
        mesh=mesh,
        in_specs=(P(None, None, "lat", "lon"), P(), P(), P(), P()),
        out_specs=P(None, None, "lat", "lon"),
        check_vma=False,
    )
```

profile of v0, /device:TPU:0, one launch (start us, length us, event | category | flops | bytes accessed | tf_op | source)
XLA Modules:
  0.0 374.6 jit_solution(14722888508883360047)
XLA Ops:
  0.0 3.0 collective-permute-start
  3.0 22.0 %collective-permute-done = f32[5,1,32,1440]{3,2,1,0:T(8,128)S(1)} collective-permute-done((f32[5,1,32,1440]{3,2,1,0:T(8,128)}, f32[5,1,32,1440]{3,2,1,0:T(8,128)S(1)}, u32[]{:S(2)}, u32[]{:S(2)}) %collective-permute-start) | collective-permute-done | bytes 921632 | tf_op jit(solution)/shard_map/ppermute | solution.py:15
  26.3 13.1 %collective-permute-done.1 = f32[5,1,32,1440]{3,2,1,0:T(8,128)S(1)} collective-permute-done((f32[5,1,32,1440]{3,2,1,0:T(8,128)S(1)}, f32[5,1,32,1440]{3,2,1,0:T(8,128)S(1)}, u32[]{:S(2)}, u32[]{:S(2)}) %collective-permute-start.1) | collective-permute-done | bytes 921632 | tf_op jit(solution)/shard_map/ppermute | solution.py:15
  40.4 22.2 %collective-permute-done.2 = f32[5,1,32,1440]{3,2,1,0:T(8,128)S(1)} collective-permute-done((f32[5,1,32,1440]{3,2,1,0:T(8,128)S(1)}, f32[5,1,32,1440]{3,2,1,0:T(8,128)S(1)}, u32[]{:S(2)}, u32[]{:S(2)}) %collective-permute-start.2) | collective-permute-done | bytes 921632 | tf_op jit(solution)/shard_map/ppermute | solution.py:15
  64.4 19.7 %collective-permute-done.3 = f32[5,1,32,1440]{3,2,1,0:T(8,128)S(1)} collective-permute-done((f32[5,1,32,1440]{3,2,1,0:T(8,128)S(1)}, f32[5,1,32,1440]{3,2,1,0:T(8,128)S(1)}, u32[]{:S(2)}, u32[]{:S(2)}) %collective-permute-start.3) | collective-permute-done | bytes 921632 | tf_op jit(solution)/shard_map/ppermute | solution.py:15
  85.2 13.6 %collective-permute-done.4 = f32[5,1,32,1440]{3,2,1,0:T(8,128)S(1)} collective-permute-done((f32[5,1,32,1440]{3,2,1,0:T(8,128)S(1)}, f32[5,1,32,1440]{3,2,1,0:T(8,128)S(1)}, u32[]{:S(2)}, u32[]{:S(2)}) %collective-permute-start.4) | collective-permute-done | bytes 921632 | tf_op jit(solution)/shard_map/ppermute | solution.py:15
  107.5 3.8 %all-to-all-start = ((f32[8,20,1440]{2,1,0:T(8,128)}), f32[8,20,1440]{2,1,0:T(8,128)S(1)}, u32[]{:S(2)}, u32[]{:S(2)}) async-start(f32[8,20,1440]{2,1,0:T(8,128)} %all_to_all.52), calls=%async_computation | async-start | bytes 2359296 | tf_op jit(solution)/shard_map/all_to_all | solution.py:152
  112.8 15.0 %all-to-all-done = f32[8,20,1440]{2,1,0:T(8,128)S(1)} async-done(((f32[8,20,1440]{2,1,0:T(8,128)}), f32[8,20,1440]{2,1,0:T(8,128)S(1)}, u32[]{:S(2)}, u32[]{:S(2)}) %all-to-all-start) | async-done | bytes 921632 | tf_op jit(solution)/shard_map/all_to_all | solution.py:152
  154.8 2.9 div.293
  157.7 4.0 %copy_select_fusion.1 = f32[20,8,1440]{2,0,1:T(8,128)} fusion(f32[20,8,1440]{2,1,0:T(8,128)} %div.293, f32[20,8,1440]{2,1,0:T(8,128)S(1)} %copy-done.2, f32[20,8,1440]{2,1,0:T(8,128)S(1)} %copy-done.3, f32[20]{0:T(128)S(1)} %get-tuple-element.18, f32[20]{0:T(128)S(1)} %get-tuple-element.19, pred[20]{0:T(512)(128)(4,1)S(1)} %dynamic-slice_compare_fusion, ...), kind=kLoop, calls=%fused_computation.69 | loop fusion | flops 1612800 | bytes 4608180 | tf_op jit(solution)/shard_map/jit(_where)/select_n | solution.py:110
  161.7 3.7 all-to-all-start.1
  166.0 16.2 %all-to-all-done.1 = f32[20,8,1440]{2,0,1:T(8,128)S(1)} async-done(((f32[20,8,1440]{2,0,1:T(8,128)}), f32[20,8,1440]{2,0,1:T(8,128)S(1)}, u32[]{:S(2)}, u32[]{:S(2)}) %all-to-all-start.1) | async-done | bytes 921632 | tf_op jit(solution)/shard_map/all_to_all | solution.py:155
  182.3 3.3 collective-permute-start.5
  188.6 19.2 %collective-permute-done.6 = f32[5,1,32,1440]{3,2,0,1:T(8,128)S(1)} collective-permute-done((f32[5,1,32,1440]{3,2,0,1:T(8,128)S(1)}, f32[5,1,32,1440]{3,2,0,1:T(8,128)S(1)}, u32[]{:S(2)}, u32[]{:S(2)}) %collective-permute-start.6) | collective-permute-done | bytes 921632 | tf_op jit(solution)/shard_map/ppermute | solution.py:15
  207.9 14.4 %collective-permute-done.7 = f32[5,1,32,1440]{3,2,0,1:T(8,128)S(1)} collective-permute-done((f32[5,1,32,1440]{3,2,0,1:T(8,128)S(1)}, f32[5,1,32,1440]{3,2,0,1:T(8,128)S(1)}, u32[]{:S(2)}, u32[]{:S(2)}) %collective-permute-start.7) | collective-permute-done | bytes 921632 | tf_op jit(solution)/shard_map/ppermute | solution.py:15
  225.4 22.2 %collective-permute-done.8 = f32[5,1,32,1440]{3,2,0,1:T(8,128)S(1)} collective-permute-done((f32[5,1,32,1440]{3,2,0,1:T(8,128)S(1)}, f32[5,1,32,1440]{3,2,0,1:T(8,128)S(1)}, u32[]{:S(2)}, u32[]{:S(2)}) %collective-permute-start.8) | collective-permute-done | bytes 921632 | tf_op jit(solution)/shard_map/ppermute | solution.py:15
  248.2 22.8 %collective-permute-done.9 = f32[5,1,32,1440]{3,2,0,1:T(8,128)S(1)} collective-permute-done((f32[5,1,32,1440]{3,2,0,1:T(8,128)S(1)}, f32[5,1,32,1440]{3,2,0,1:T(8,128)S(1)}, u32[]{:S(2)}, u32[]{:S(2)}) %collective-permute-start.9) | collective-permute-done | bytes 921632 | tf_op jit(solution)/shard_map/ppermute | solution.py:15
  271.4 14.3 %collective-permute-done.10 = f32[5,1,32,1440]{3,2,0,1:T(8,128)S(1)} collective-permute-done((f32[5,1,32,1440]{3,2,0,1:T(8,128)S(1)}, f32[5,1,32,1440]{3,2,0,1:T(8,128)S(1)}, u32[]{:S(2)}, u32[]{:S(2)}) %collective-permute-start.10) | collective-permute-done | bytes 921632 | tf_op jit(solution)/shard_map/ppermute | solution.py:15
  294.5 3.8 %all-to-all-start.2 = ((f32[8,20,1440]{2,1,0:T(8,128)}), f32[8,20,1440]{2,1,0:T(8,128)S(1)}, u32[]{:S(2)}, u32[]{:S(2)}) async-start(f32[8,20,1440]{2,1,0:T(8,128)} %all_to_all.59), calls=%async_computation.2 | async-start | bytes 2359296 | tf_op jit(solution)/shard_map/all_to_all | solution.py:152
  298.4 16.3 %all-to-all-done.2 = f32[8,20,1440]{2,1,0:T(8,128)S(1)} async-done(((f32[8,20,1440]{2,1,0:T(8,128)}), f32[8,20,1440]{2,1,0:T(8,128)S(1)}, u32[]{:S(2)}, u32[]{:S(2)}) %all-to-all-start.2) | async-done | bytes 921632 | tf_op jit(solution)/shard_map/all_to_all | solution.py:152
  341.6 2.9 div.296
  344.5 2.9 copy_select_fusion
  347.5 19.2 %all_to_all.70 = f32[20,8,1440]{2,0,1:T(8,128)S(1)} all-to-all(f32[20,8,1440]{2,0,1:T(8,128)S(1)} %copy_select_fusion), channel_id=1, replica_groups=mesh['lon'=8,'lat'=4] {'lon'}, dimensions={1} | all-to-all | bytes 1843200 | tf_op jit(solution)/shard_map/all_to_all | solution.py:155
  366.8 4.0 %collective-permute-start.11 = (f32[5,1,2,1440]{3,2,0,1:T(2,128)S(1)}, f32[5,1,2,1440]{3,2,0,1:T(2,128)S(1)}, u32[]{:S(2)}, u32[]{:S(2)}) collective-permute-start(f32[5,1,2,1440]{3,2,0,1:T(2,128)S(1)} %slice.367), channel_id=1, source_target_pairs={{0,1},{1,2},{2,3},{4,5},{5,6},{6,7},{8,9},{9,10},{10,11},{12,13},{... | collective-permute-start | bytes 172808 | tf_op jit(solution)/shard_map/ppermute | solution.py:21
  (188 shorter events, 88.9 us)
Async XLA Ops:
  0.0 24.9 %collective-permute-start = (f32[5,1,32,1440]{3,2,1,0:T(8,128)}, f32[5,1,32,1440]{3,2,1,0:T(8,128)S(1)}, u32[]{:S(2)}, u32[]{:S(2)}) collective-permute-start(f32[5,1,32,1440]{3,2,1,0:T(8,128)} %param.5), channel_id=1, source_target_pairs={{0,16},{4,20},{8,24},{12,28},{16,0},{20,4},{24,8},{28,12},{1,17},{... | collective-permute-start | bytes 2764808 | tf_op jit(solution)/shard_map/ppermute | solution.py:15
  24.9 14.4 %collective-permute-start.1 = (f32[5,1,32,1440]{3,2,1,0:T(8,128)S(1)}, f32[5,1,32,1440]{3,2,1,0:T(8,128)S(1)}, u32[]{:S(2)}, u32[]{:S(2)}) collective-permute-start(f32[5,1,32,1440]{3,2,1,0:T(8,128)S(1)} %collective-permute-done), channel_id=1, source_target_pairs={{0,4},{4,8},{8,12},{12,16},{16,20},{20,24},{24,28},{28,0},{1,5},{5... | collective-permute-start | bytes 2764808 | tf_op jit(solution)/shard_map/ppermute | solution.py:15
  39.6 23.1 %collective-permute-start.2 = (f32[5,1,32,1440]{3,2,1,0:T(8,128)S(1)}, f32[5,1,32,1440]{3,2,1,0:T(8,128)S(1)}, u32[]{:S(2)}, u32[]{:S(2)}) collective-permute-start(f32[5,1,32,1440]{3,2,1,0:T(8,128)S(1)} %broadcast_select_fusion), channel_id=1, source_target_pairs={{0,8},{4,12},{8,16},{12,20},{16,24},{20,28},{24,0},{28,4},{1,9},{5... | collective-permute-start | bytes 2764808 | tf_op jit(solution)/shard_map/ppermute | solution.py:15
  62.8 21.5 %copy-start.12 = (s32[128]{0:T(128)S(1)}, s32[128]{0:T(128)}, u32[]{:S(2)}) copy-start(s32[128]{0:T(128)} %param.9) | copy-start | bytes 1540
  62.8 21.6 %copy-start.10 = (f32[2,1,128]{2,1,0:T(1,128)S(1)}, f32[2,1,128]{2,1,0:T(1,128)}, u32[]{:S(2)}) copy-start(f32[2,1,128]{2,1,0:T(1,128)} %param.6) | copy-start | bytes 3076
  62.8 21.3 %collective-permute-start.3 = (f32[5,1,32,1440]{3,2,1,0:T(8,128)S(1)}, f32[5,1,32,1440]{3,2,1,0:T(8,128)S(1)}, u32[]{:S(2)}, u32[]{:S(2)}) collective-permute-start(f32[5,1,32,1440]{3,2,1,0:T(8,128)S(1)} %broadcast_select_fusion.1), channel_id=1, source_target_pairs={{0,16},{4,20},{8,24},{12,28},{16,0},{20,4},{24,8},{28,12},{1,17},{... | collective-permute-start | bytes 2764808 | tf_op jit(solution)/shard_map/ppermute | solution.py:15
  84.3 14.5 %collective-permute-start.4 = (f32[5,1,32,1440]{3,2,1,0:T(8,128)S(1)}, f32[5,1,32,1440]{3,2,1,0:T(8,128)S(1)}, u32[]{:S(2)}, u32[]{:S(2)}) collective-permute-start(f32[5,1,32,1440]{3,2,1,0:T(8,128)S(1)} %broadcast_select_fusion.2), channel_id=1, source_target_pairs={{0,4},{4,8},{8,12},{12,16},{16,20},{20,24},{24,28},{28,0},{1,5},{5... | collective-permute-start | bytes 2764808 | tf_op jit(solution)/shard_map/ppermute | solution.py:15
  107.5 20.3 %all-to-all-start = ((f32[8,20,1440]{2,1,0:T(8,128)}), f32[8,20,1440]{2,1,0:T(8,128)S(1)}, u32[]{:S(2)}, u32[]{:S(2)}) async-start(f32[8,20,1440]{2,1,0:T(8,128)} %all_to_all.52), calls=%async_computation | async-start | bytes 2359296 | tf_op jit(solution)/shard_map/all_to_all | solution.py:152
  154.8 2.9 copy-start.3
  161.7 3.7 copy-start.11
  161.7 20.4 %all-to-all-start.1 = ((f32[20,8,1440]{2,0,1:T(8,128)}), f32[20,8,1440]{2,0,1:T(8,128)S(1)}, u32[]{:S(2)}, u32[]{:S(2)}) async-start(f32[20,8,1440]{2,0,1:T(8,128)} %copy_select_fusion.1), calls=%async_computation.1 | async-start | bytes 2359296 | tf_op jit(solution)/shard_map/all_to_all | solution.py:155
  182.3 5.1 %collective-permute-start.5 = (f32[5,1,2,1440]{3,2,0,1:T(2,128)S(1)}, f32[5,1,2,1440]{3,2,0,1:T(2,128)S(1)}, u32[]{:S(2)}, u32[]{:S(2)}) collective-permute-start(f32[5,1,2,1440]{3,2,0,1:T(2,128)S(1)} %slice.334), channel_id=1, source_target_pairs={{0,1},{1,2},{2,3},{4,5},{5,6},{6,7},{8,9},{9,10},{10,11},{12,13},{... | collective-permute-start | bytes 172808 | tf_op jit(solution)/shard_map/ppermute | solution.py:21
  187.8 20.1 %copy-start.7 = (s32[32]{0:T(128)S(1)}, s32[32]{0:T(128)}, u32[]{:S(2)}) copy-start(s32[32]{0:T(128)} %get-tuple-element.57) | copy-start | bytes 388
  188.0 19.8 %collective-permute-start.6 = (f32[5,1,32,1440]{3,2,0,1:T(8,128)S(1)}, f32[5,1,32,1440]{3,2,0,1:T(8,128)S(1)}, u32[]{:S(2)}, u32[]{:S(2)}) collective-permute-start(f32[5,1,32,1440]{3,2,0,1:T(8,128)S(1)} %slice_subtract_fusion.1), channel_id=1, source_target_pairs={{0,16},{4,20},{8,24},{12,28},{16,0},{20,4},{24,8},{28,12},{1,17},{... | collective-permute-start | bytes 2764808 | tf_op jit(solution)/shard_map/ppermute | solution.py:15
  207.9 14.4 %collective-permute-start.7 = (f32[5,1,32,1440]{3,2,0,1:T(8,128)S(1)}, f32[5,1,32,1440]{3,2,0,1:T(8,128)S(1)}, u32[]{:S(2)}, u32[]{:S(2)}) collective-permute-start(f32[5,1,32,1440]{3,2,0,1:T(8,128)S(1)} %collective-permute-done.6), channel_id=1, source_target_pairs={{0,4},{4,8},{8,12},{12,16},{16,20},{20,24},{24,28},{28,0},{1,5},{5... | collective-permute-start | bytes 2764808 | tf_op jit(solution)/shard_map/ppermute | solution.py:15
  222.5 25.1 %collective-permute-start.8 = (f32[5,1,32,1440]{3,2,0,1:T(8,128)S(1)}, f32[5,1,32,1440]{3,2,0,1:T(8,128)S(1)}, u32[]{:S(2)}, u32[]{:S(2)}) collective-permute-start(f32[5,1,32,1440]{3,2,0,1:T(8,128)S(1)} %broadcast_select_fusion.3), channel_id=1, source_target_pairs={{0,8},{4,12},{8,16},{12,20},{16,24},{20,28},{24,0},{28,4},{1,9},{5... | collective-permute-start | bytes 2764808 | tf_op jit(solution)/shard_map/ppermute | solution.py:15
  247.8 23.5 %copy-start.8 = (s32[32]{0:T(128)S(1)}, s32[32]{0:T(128)}, u32[]{:S(2)}) copy-start(s32[32]{0:T(128)} %get-tuple-element.56) | copy-start | bytes 388
  247.8 23.3 %collective-permute-start.9 = (f32[5,1,32,1440]{3,2,0,1:T(8,128)S(1)}, f32[5,1,32,1440]{3,2,0,1:T(8,128)S(1)}, u32[]{:S(2)}, u32[]{:S(2)}) collective-permute-start(f32[5,1,32,1440]{3,2,0,1:T(8,128)S(1)} %broadcast_select_fusion.4), channel_id=1, source_target_pairs={{0,16},{4,20},{8,24},{12,28},{16,0},{20,4},{24,8},{28,12},{1,17},{... | collective-permute-start | bytes 2764808 | tf_op jit(solution)/shard_map/ppermute | solution.py:15
  271.3 14.5 %collective-permute-start.10 = (f32[5,1,32,1440]{3,2,0,1:T(8,128)S(1)}, f32[5,1,32,1440]{3,2,0,1:T(8,128)S(1)}, u32[]{:S(2)}, u32[]{:S(2)}) collective-permute-start(f32[5,1,32,1440]{3,2,0,1:T(8,128)S(1)} %broadcast_select_fusion.5), channel_id=1, source_target_pairs={{0,4},{4,8},{8,12},{12,16},{16,20},{20,24},{24,28},{28,0},{1,5},{5... | collective-permute-start | bytes 2764808 | tf_op jit(solution)/shard_map/ppermute | solution.py:15
  293.3 5.0 %copy-start.6 = (f32[32]{0:T(128)S(1)}, f32[32]{0:T(128)}, u32[]{:S(2)}) copy-start(f32[32]{0:T(128)} %get-tuple-element.61) | copy-start | bytes 388
  294.5 20.3 %all-to-all-start.2 = ((f32[8,20,1440]{2,1,0:T(8,128)}), f32[8,20,1440]{2,1,0:T(8,128)S(1)}, u32[]{:S(2)}, u32[]{:S(2)}) async-start(f32[8,20,1440]{2,1,0:T(8,128)} %all_to_all.59), calls=%async_computation.2 | async-start | bytes 2359296 | tf_op jit(solution)/shard_map/all_to_all | solution.py:152
  341.6 2.9 copy-start.1
  347.4 23.3 %copy-start.9 = (f32[1,128]{1,0:T(1,128)S(1)}, f32[1,128]{1,0:T(1,128)}, u32[]{:S(2)}) copy-start(f32[1,128]{1,0:T(1,128)} %get-tuple-element.23) | copy-start | bytes 1540
  366.8 5.8 %collective-permute-start.11 = (f32[5,1,2,1440]{3,2,0,1:T(2,128)S(1)}, f32[5,1,2,1440]{3,2,0,1:T(2,128)S(1)}, u32[]{:S(2)}, u32[]{:S(2)}) collective-permute-start(f32[5,1,2,1440]{3,2,0,1:T(2,128)S(1)} %slice.367), channel_id=1, source_target_pairs={{0,1},{1,2},{2,3},{4,5},{5,6},{6,7},{8,9},{9,10},{10,11},{12,13},{... | collective-permute-start | bytes 172808 | tf_op jit(solution)/shard_map/ppermute | solution.py:21
  (6 other events, 13.8 us)
where the time goes:
time: 381 us; the launch traced here: 375 us
  waiting for transfers between devices  234 us (61%)
  matrix products  31.4 us (8%)
  local copies, waits for them, and re-layouts  30.5 us (8%)
  other arithmetic  29.7 us (8%)
  starting transfers between devices  27.9 us (7%)
  blocking collectives  19.2 us (5%)
    ppermute x10, waiting for transfers between devices, passed_along(): lax.ppermute(x, axis, [(i, (i + by) % devices) for i in range(devices)])  183 us
    all_to_all x2, waiting for transfers between devices, body(): whole = lax.all_to_all(flat, 'lon', split_axis=0, concat_axis=1, tiled=True)  31.3 us
    all_to_all x1, blocking collectives, body(): lax.all_to_all(whole, 'lon', split_axis=1, concat_axis=0, tiled=True)  19.2 us
    all_to_all x1, waiting for transfers between devices, body(): lax.all_to_all(whole, 'lon', split_axis=1, concat_axis=0, tiled=True)  16.2 us
    select_n x22, other arithmetic, roll_digits(): values = jnp.where(taken, moved, values)  11.1 us
    ppermute x10, starting transfers between devices, passed_along(): lax.ppermute(x, axis, [(i, (i + by) % devices) for i in range(devices)])  9.47 us
  transfers between devices with their start and end apart: 15, of which 15 were waited for; matrix products, arithmetic and copies ran while one was open for 1% of the time, Pallas kernels for 0%

commit v1 on v0

--- a/solution.py
+++ b/solution.py
@@ -152,7 +152,19 @@
         whole = lax.all_to_all(flat, "lon", split_axis=0, concat_axis=1, tiled=True)
         whole = zonal_fraction(whole, my_rows(fractions)[:, None])
         whole = polar_smooth(whole, row_lats, row_marks, lat_cells, lat_total)
-        blocks = lax.all_to_all(whole, "lon", split_axis=1, concat_axis=0, tiled=True)
+        ways, here = (lax.axis_size("lon"), lax.axis_index("lon"))
+        width = whole.shape[1] // ways
+        shape = list(whole.shape)
+        shape[1] = width
+        height = shape[0]
+        shape[0] = height * ways
+        full = jnp.zeros(shape, whole.dtype)
+        for mask in range(ways):
+            part = lax.dynamic_slice_in_dim(whole, (here ^ mask) * width, width, axis=1)
+            if mask:
+                part = lax.ppermute(part, "lon", [(d, d ^ mask) for d in range(ways)])
+            full = lax.dynamic_update_slice_in_dim(full, part, (here ^ mask) * height, axis=0)
+        blocks = full
         state = blocks.reshape(n_fields, n_levels, lat_cells, lon_cells)
         state = meridional(state, frac_y[substep], first_row)
     return state

time: 381 us -> 367 us (0.963)
  blocking collectives: 19.2 us -> 0 us
  local copies, waits for them, and re-layouts: 30.5 us -> 39.3 us
  other arithmetic: 29.7 us -> 25 us
    all_to_all x1 -> x0, blocking collectives: 19.2 us -> none  [body(): lax.all_to_all(whole, 'lon', split_axis=1, concat_axis=0, tiled=True)]
    dynamic_update_slice x0 -> x16, local copies, waits for them, and re-layouts: none -> 17.6 us  [body(): lax.dynamic_update_slice_in_dim(full, part, (here ^ mask) * height, axis=0)]
    all_to_all x1 -> x0, waiting for transfers between devices: 16.2 us -> none  [body(): lax.all_to_all(whole, 'lon', split_axis=1, concat_axis=0, tiled=True)]
    ppermute x0 -> x14, waiting for transfers between devices: none -> 13.2 us  [body(): part = lax.ppermute(part, 'lon', [(d, d ^ mask) for d in range(ways)])]
    ppermute x0 -> x14, starting transfers between devices: none -> 8.45 us  [body(): part = lax.ppermute(part, 'lon', [(d, d ^ mask) for d in range(ways)])]
    select_n x2, other arithmetic: 6.9 us -> 0.83 us  [polar_smooth(): return jnp.where((marks == 1)[:, None], result, whole)]
    div x2 -> x0, local copies, waits for them, and re-layouts: 5.86 us -> none  [polar_smooth(): result = result.reshape(row_count, lon_total) / lon_total]
  transfers between devices with their start and end apart: 15 -> 28, of which waited for: 15 -> 18; matrix products, arithmetic and copies ran while one was open for 1% -> 5% of each run, Pallas kernels for 0% -> 0%
where the time goes in v1:
time: 367 us; the launch traced here: 360 us
  waiting for transfers between devices  233 us (63%)
  local copies, waits for them, and re-layouts  39.3 us (11%)
  starting transfers between devices  31.7 us (9%)
  matrix products  29.5 us (8%)
  other arithmetic  25 us (7%)
    ppermute x10, waiting for transfers between devices, passed_along(): lax.ppermute(x, axis, [(i, (i + by) % devices) for i in range(devices)])  185 us
    all_to_all x2, waiting for transfers between devices, body(): whole = lax.all_to_all(flat, 'lon', split_axis=0, concat_axis=1, tiled=True)  31.9 us
    dynamic_update_slice x16, local copies, waits for them, and re-layouts, body(): lax.dynamic_update_slice_in_dim(full, part, (here ^ mask) * height, axis=0)  17.6 us
    ppermute x14, waiting for transfers between devices, body(): part = lax.ppermute(part, 'lon', [(d, d ^ mask) for d in range(ways)])  13.2 us
    select_n x22, other arithmetic, roll_digits(): values = jnp.where(taken, moved, values)  11.1 us
    ppermute x14, starting transfers between devices, body(): part = lax.ppermute(part, 'lon', [(d, d ^ mask) for d in range(ways)])  8.45 us
    ppermute x10, starting transfers between devices, passed_along(): lax.ppermute(x, axis, [(i, (i + by) % devices) for i in range(devices)])  8.01 us
    ppermute x2, starting transfers between devices, passed_along_2(): return lax.ppermute(block, axis, route)  7.7 us
  transfers between devices with their start and end apart: 28, of which 18 were waited for; matrix products, arithmetic and copies ran while one was open for 5% of the time, Pallas kernels for 0%

profile of v1, /device:TPU:0, one launch (start us, length us, event | category | flops | bytes accessed | tf_op | source)
XLA Modules:
  0.0 360.5 jit_solution(18100839967813760847)
XLA Ops:
  0.0 3.0 collective-permute-start
  3.0 22.0 %collective-permute-done = f32[5,1,32,1440]{3,2,1,0:T(8,128)S(1)} collective-permute-done((f32[5,1,32,1440]{3,2,1,0:T(8,128)}, f32[5,1,32,1440]{3,2,1,0:T(8,128)S(1)}, u32[]{:S(2)}, u32[]{:S(2)}) %collective-permute-start) | collective-permute-done | bytes 921632 | tf_op jit(solution)/shard_map/ppermute | solution.py:15
  25.7 13.6 %collective-permute-done.1 = f32[5,1,32,1440]{3,2,1,0:T(8,128)S(1)} collective-permute-done((f32[5,1,32,1440]{3,2,1,0:T(8,128)S(1)}, f32[5,1,32,1440]{3,2,1,0:T(8,128)S(1)}, u32[]{:S(2)}, u32[]{:S(2)}) %collective-permute-start.1) | collective-permute-done | bytes 921632 | tf_op jit(solution)/shard_map/ppermute | solution.py:15
  40.4 22.2 %collective-permute-done.2 = f32[5,1,32,1440]{3,2,1,0:T(8,128)S(1)} collective-permute-done((f32[5,1,32,1440]{3,2,1,0:T(8,128)S(1)}, f32[5,1,32,1440]{3,2,1,0:T(8,128)S(1)}, u32[]{:S(2)}, u32[]{:S(2)}) %collective-permute-start.2) | collective-permute-done | bytes 921632 | tf_op jit(solution)/shard_map/ppermute | solution.py:15
  64.4 19.7 %collective-permute-done.3 = f32[5,1,32,1440]{3,2,1,0:T(8,128)S(1)} collective-permute-done((f32[5,1,32,1440]{3,2,1,0:T(8,128)S(1)}, f32[5,1,32,1440]{3,2,1,0:T(8,128)S(1)}, u32[]{:S(2)}, u32[]{:S(2)}) %collective-permute-start.3) | collective-permute-done | bytes 921632 | tf_op jit(solution)/shard_map/ppermute | solution.py:15
  84.7 14.1 %collective-permute-done.4 = f32[5,1,32,1440]{3,2,1,0:T(8,128)S(1)} collective-permute-done((f32[5,1,32,1440]{3,2,1,0:T(8,128)S(1)}, f32[5,1,32,1440]{3,2,1,0:T(8,128)S(1)}, u32[]{:S(2)}, u32[]{:S(2)}) %collective-permute-start.4) | collective-permute-done | bytes 921632 | tf_op jit(solution)/shard_map/ppermute | solution.py:15
  107.5 3.8 %all-to-all-start = ((f32[8,20,1440]{2,1,0:T(8,128)}), f32[8,20,1440]{2,1,0:T(8,128)S(1)}, u32[]{:S(2)}, u32[]{:S(2)}) async-start(f32[8,20,1440]{2,1,0:T(8,128)} %all_to_all.32), calls=%async_computation | async-start | bytes 2359296 | tf_op jit(solution)/shard_map/all_to_all | solution.py:152
  112.3 15.5 %all-to-all-done = f32[8,20,1440]{2,1,0:T(8,128)S(1)} async-done(((f32[8,20,1440]{2,1,0:T(8,128)}), f32[8,20,1440]{2,1,0:T(8,128)S(1)}, u32[]{:S(2)}, u32[]{:S(2)}) %all-to-all-start) | async-done | bytes 921632 | tf_op jit(solution)/shard_map/all_to_all | solution.py:152
  132.2 2.4 concatenate.843
  135.8 2.3 multiply_subtract_fusion.3
  158.9 2.5 collective-permute-done.6
  167.6 4.0 %collective-permute-done.9 = f32[20,1440]{1,0:T(8,128)S(1)} collective-permute-done((f32[20,1440]{1,0:T(8,128)S(1)}, f32[20,1440]{1,0:T(8,128)S(1)}, u32[]{:S(2)}, u32[]{:S(2)}) %collective-permute-start.9) | collective-permute-done | bytes 115232 | tf_op jit(solution)/shard_map/ppermute | solution.py:165
  174.5 3.3 collective-permute-start.12
  181.5 22.0 %collective-permute-done.13 = f32[5,1,32,1440]{3,2,0,1:T(8,128)S(1)} collective-permute-done((f32[5,1,32,1440]{3,2,0,1:T(8,128)S(1)}, f32[5,1,32,1440]{3,2,0,1:T(8,128)S(1)}, u32[]{:S(2)}, u32[]{:S(2)}) %collective-permute-start.13) | collective-permute-done | bytes 921632 | tf_op jit(solution)/shard_map/ppermute | solution.py:15
  203.5 14.4 %collective-permute-done.14 = f32[5,1,32,1440]{3,2,0,1:T(8,128)S(1)} collective-permute-done((f32[5,1,32,1440]{3,2,0,1:T(8,128)S(1)}, f32[5,1,32,1440]{3,2,0,1:T(8,128)S(1)}, u32[]{:S(2)}, u32[]{:S(2)}) %collective-permute-start.14) | collective-permute-done | bytes 921632 | tf_op jit(solution)/shard_map/ppermute | solution.py:15
  218.6 22.2 %collective-permute-done.15 = f32[5,1,32,1440]{3,2,0,1:T(8,128)S(1)} collective-permute-done((f32[5,1,32,1440]{3,2,0,1:T(8,128)S(1)}, f32[5,1,32,1440]{3,2,0,1:T(8,128)S(1)}, u32[]{:S(2)}, u32[]{:S(2)}) %collective-permute-start.15) | collective-permute-done | bytes 921632 | tf_op jit(solution)/shard_map/ppermute | solution.py:15
  241.6 20.3 %collective-permute-done.16 = f32[5,1,32,1440]{3,2,0,1:T(8,128)S(1)} collective-permute-done((f32[5,1,32,1440]{3,2,0,1:T(8,128)S(1)}, f32[5,1,32,1440]{3,2,0,1:T(8,128)S(1)}, u32[]{:S(2)}, u32[]{:S(2)}) %collective-permute-start.16) | collective-permute-done | bytes 921632 | tf_op jit(solution)/shard_map/ppermute | solution.py:15
  262.4 14.3 %collective-permute-done.17 = f32[5,1,32,1440]{3,2,0,1:T(8,128)S(1)} collective-permute-done((f32[5,1,32,1440]{3,2,0,1:T(8,128)S(1)}, f32[5,1,32,1440]{3,2,0,1:T(8,128)S(1)}, u32[]{:S(2)}, u32[]{:S(2)}) %collective-permute-start.17) | collective-permute-done | bytes 921632 | tf_op jit(solution)/shard_map/ppermute | solution.py:15
  285.4 3.8 %all-to-all-start.1 = ((f32[8,20,1440]{2,1,0:T(8,128)}), f32[8,20,1440]{2,1,0:T(8,128)S(1)}, u32[]{:S(2)}, u32[]{:S(2)}) async-start(f32[8,20,1440]{2,1,0:T(8,128)} %all_to_all.37), calls=%async_computation.1 | async-start | bytes 2359296 | tf_op jit(solution)/shard_map/all_to_all | solution.py:152
  289.3 16.4 %all-to-all-done.1 = f32[8,20,1440]{2,1,0:T(8,128)S(1)} async-done(((f32[8,20,1440]{2,1,0:T(8,128)}), f32[8,20,1440]{2,1,0:T(8,128)S(1)}, u32[]{:S(2)}, u32[]{:S(2)}) %all-to-all-start.1) | async-done | bytes 921632 | tf_op jit(solution)/shard_map/all_to_all | solution.py:152
  310.1 2.4 concatenate.861
  336.6 2.6 collective-permute-done.19
  345.3 4.0 %collective-permute-done.22 = f32[20,1440]{1,0:T(8,128)S(1)} collective-permute-done((f32[20,1440]{1,0:T(8,128)S(1)}, f32[20,1440]{1,0:T(8,128)S(1)}, u32[]{:S(2)}, u32[]{:S(2)}) %collective-permute-start.22) | collective-permute-done | bytes 115232 | tf_op jit(solution)/shard_map/ppermute | solution.py:165
  352.2 4.4 %collective-permute-start.25 = (f32[5,1,2,1440]{3,2,1,0:T(2,128)S(1)}, f32[5,1,2,1440]{3,2,1,0:T(2,128)S(1)}, u32[]{:S(2)}, u32[]{:S(2)}) collective-permute-start(f32[5,1,2,1440]{3,2,1,0:T(2,128)S(1)} %slice.367), channel_id=1, source_target_pairs={{0,1},{1,2},{2,3},{4,5},{5,6},{6,7},{8,9},{9,10},{10,11},{12,13},{... | collective-permute-start | bytes 172808 | tf_op jit(solution)/shard_map/ppermute | solution.py:21
  (205 shorter events, 103.8 us)
Async XLA Ops:
  0.0 24.9 %collective-permute-start = (f32[5,1,32,1440]{3,2,1,0:T(8,128)}, f32[5,1,32,1440]{3,2,1,0:T(8,128)S(1)}, u32[]{:S(2)}, u32[]{:S(2)}) collective-permute-start(f32[5,1,32,1440]{3,2,1,0:T(8,128)} %param.5), channel_id=1, source_target_pairs={{0,16},{4,20},{8,24},{12,28},{16,0},{20,4},{24,8},{28,12},{1,17},{... | collective-permute-start | bytes 2764808 | tf_op jit(solution)/shard_map/ppermute | solution.py:15
  24.9 14.4 %collective-permute-start.1 = (f32[5,1,32,1440]{3,2,1,0:T(8,128)S(1)}, f32[5,1,32,1440]{3,2,1,0:T(8,128)S(1)}, u32[]{:S(2)}, u32[]{:S(2)}) collective-permute-start(f32[5,1,32,1440]{3,2,1,0:T(8,128)S(1)} %collective-permute-done), channel_id=1, source_target_pairs={{0,4},{4,8},{8,12},{12,16},{16,20},{20,24},{24,28},{28,0},{1,5},{5... | collective-permute-start | bytes 2764808 | tf_op jit(solution)/shard_map/ppermute | solution.py:15
  39.6 23.1 %collective-permute-start.2 = (f32[5,1,32,1440]{3,2,1,0:T(8,128)S(1)}, f32[5,1,32,1440]{3,2,1,0:T(8,128)S(1)}, u32[]{:S(2)}, u32[]{:S(2)}) collective-permute-start(f32[5,1,32,1440]{3,2,1,0:T(8,128)S(1)} %broadcast_select_fusion), channel_id=1, source_target_pairs={{0,8},{4,12},{8,16},{12,20},{16,24},{20,28},{24,0},{28,4},{1,9},{5... | collective-permute-start | bytes 2764808 | tf_op jit(solution)/shard_map/ppermute | solution.py:15
  62.8 21.3 %collective-permute-start.3 = (f32[5,1,32,1440]{3,2,1,0:T(8,128)S(1)}, f32[5,1,32,1440]{3,2,1,0:T(8,128)S(1)}, u32[]{:S(2)}, u32[]{:S(2)}) collective-permute-start(f32[5,1,32,1440]{3,2,1,0:T(8,128)S(1)} %broadcast_select_fusion.1), channel_id=1, source_target_pairs={{0,16},{4,20},{8,24},{12,28},{16,0},{20,4},{24,8},{28,12},{1,17},{... | collective-permute-start | bytes 2764808 | tf_op jit(solution)/shard_map/ppermute | solution.py:15
  84.3 14.5 %collective-permute-start.4 = (f32[5,1,32,1440]{3,2,1,0:T(8,128)S(1)}, f32[5,1,32,1440]{3,2,1,0:T(8,128)S(1)}, u32[]{:S(2)}, u32[]{:S(2)}) collective-permute-start(f32[5,1,32,1440]{3,2,1,0:T(8,128)S(1)} %broadcast_select_fusion.2), channel_id=1, source_target_pairs={{0,4},{4,8},{8,12},{12,16},{16,20},{20,24},{24,28},{28,0},{1,5},{5... | collective-permute-start | bytes 2764808 | tf_op jit(solution)/shard_map/ppermute | solution.py:15
  107.5 20.3 %all-to-all-start = ((f32[8,20,1440]{2,1,0:T(8,128)}), f32[8,20,1440]{2,1,0:T(8,128)S(1)}, u32[]{:S(2)}, u32[]{:S(2)}) async-start(f32[8,20,1440]{2,1,0:T(8,128)} %all_to_all.32), calls=%async_computation | async-start | bytes 2359296 | tf_op jit(solution)/shard_map/all_to_all | solution.py:152
  154.7 6.7 %collective-permute-start.6 = (f32[20,1440]{1,0:T(8,128)S(1)}, f32[20,1440]{1,0:T(8,128)S(1)}, u32[]{:S(2)}, u32[]{:S(2)}) collective-permute-start(f32[20,1440]{1,0:T(8,128)S(1)} %get-tuple-element.36), channel_id=1, source_target_pairs={{0,8},{4,12},{8,0},{12,4},{16,24},{20,28},{24,16},{28,20},{1,9},{5... | collective-permute-start | bytes 345608 | tf_op jit(solution)/shard_map/ppermute | solution.py:165
  155.3 9.8 %collective-permute-start.7 = (f32[20,1440]{1,0:T(8,128)S(1)}, f32[20,1440]{1,0:T(8,128)S(1)}, u32[]{:S(2)}, u32[]{:S(2)}) collective-permute-start(f32[20,1440]{1,0:T(8,128)S(1)} %get-tuple-element.35), channel_id=1, source_target_pairs={{0,12},{4,8},{8,4},{12,0},{16,28},{20,24},{24,20},{28,16},{1,13},{... | collective-permute-start | bytes 345608 | tf_op jit(solution)/shard_map/ppermute | solution.py:165
  156.6 9.8 %collective-permute-start.8 = (f32[20,1440]{1,0:T(8,128)S(1)}, f32[20,1440]{1,0:T(8,128)S(1)}, u32[]{:S(2)}, u32[]{:S(2)}) collective-permute-start(f32[20,1440]{1,0:T(8,128)S(1)} %get-tuple-element.34), channel_id=1, source_target_pairs={{0,16},{4,20},{8,24},{12,28},{16,0},{20,4},{24,8},{28,12},{1,17},{... | collective-permute-start | bytes 345608 | tf_op jit(solution)/shard_map/ppermute | solution.py:165
  157.1 14.5 %collective-permute-start.9 = (f32[20,1440]{1,0:T(8,128)S(1)}, f32[20,1440]{1,0:T(8,128)S(1)}, u32[]{:S(2)}, u32[]{:S(2)}) collective-permute-start(f32[20,1440]{1,0:T(8,128)S(1)} %get-tuple-element.33), channel_id=1, source_target_pairs={{0,20},{4,16},{8,28},{12,24},{16,4},{20,0},{24,12},{28,8},{1,21},{... | collective-permute-start | bytes 345608 | tf_op jit(solution)/shard_map/ppermute | solution.py:165
  158.3 14.4 %collective-permute-start.10 = (f32[20,1440]{1,0:T(8,128)S(1)}, f32[20,1440]{1,0:T(8,128)S(1)}, u32[]{:S(2)}, u32[]{:S(2)}) collective-permute-start(f32[20,1440]{1,0:T(8,128)S(1)} %get-tuple-element.32), channel_id=1, source_target_pairs={{0,24},{4,28},{8,16},{12,20},{16,8},{20,12},{24,0},{28,4},{1,25},{... | collective-permute-start | bytes 345608 | tf_op jit(solution)/shard_map/ppermute | solution.py:165
  161.4 12.3 %collective-permute-start.11 = (f32[20,1440]{1,0:T(8,128)S(1)}, f32[20,1440]{1,0:T(8,128)S(1)}, u32[]{:S(2)}, u32[]{:S(2)}) collective-permute-start(f32[20,1440]{1,0:T(8,128)S(1)} %get-tuple-element.31), channel_id=1, source_target_pairs={{0,28},{4,24},{8,20},{12,16},{16,12},{20,8},{24,4},{28,0},{1,29},{... | collective-permute-start | bytes 345608 | tf_op jit(solution)/shard_map/ppermute | solution.py:165
  180.3 23.2 %collective-permute-start.13 = (f32[5,1,32,1440]{3,2,0,1:T(8,128)S(1)}, f32[5,1,32,1440]{3,2,0,1:T(8,128)S(1)}, u32[]{:S(2)}, u32[]{:S(2)}) collective-permute-start(f32[5,1,32,1440]{3,2,0,1:T(8,128)S(1)} %slice_subtract_fusion.1), channel_id=1, source_target_pairs={{0,16},{4,20},{8,24},{12,28},{16,0},{20,4},{24,8},{28,12},{1,17},{... | collective-permute-start | bytes 2764808 | tf_op jit(solution)/shard_map/ppermute | solution.py:15
  203.5 14.4 %collective-permute-start.14 = (f32[5,1,32,1440]{3,2,0,1:T(8,128)S(1)}, f32[5,1,32,1440]{3,2,0,1:T(8,128)S(1)}, u32[]{:S(2)}, u32[]{:S(2)}) collective-permute-start(f32[5,1,32,1440]{3,2,0,1:T(8,128)S(1)} %collective-permute-done.13), channel_id=1, source_target_pairs={{0,4},{4,8},{8,12},{12,16},{16,20},{20,24},{24,28},{28,0},{1,5},{5... | collective-permute-start | bytes 2764808 | tf_op jit(solution)/shard_map/ppermute | solution.py:15
  218.1 22.6 %collective-permute-start.15 = (f32[5,1,32,1440]{3,2,0,1:T(8,128)S(1)}, f32[5,1,32,1440]{3,2,0,1:T(8,128)S(1)}, u32[]{:S(2)}, u32[]{:S(2)}) collective-permute-start(f32[5,1,32,1440]{3,2,0,1:T(8,128)S(1)} %broadcast_select_fusion.3), channel_id=1, source_target_pairs={{0,8},{4,12},{8,16},{12,20},{16,24},{20,28},{24,0},{28,4},{1,9},{5... | collective-permute-start | bytes 2764808 | tf_op jit(solution)/shard_map/ppermute | solution.py:15
  241.0 20.9 %collective-permute-start.16 = (f32[5,1,32,1440]{3,2,0,1:T(8,128)S(1)}, f32[5,1,32,1440]{3,2,0,1:T(8,128)S(1)}, u32[]{:S(2)}, u32[]{:S(2)}) collective-permute-start(f32[5,1,32,1440]{3,2,0,1:T(8,128)S(1)} %broadcast_select_fusion.4), channel_id=1, source_target_pairs={{0,16},{4,20},{8,24},{12,28},{16,0},{20,4},{24,8},{28,12},{1,17},{... | collective-permute-start | bytes 2764808 | tf_op jit(solution)/shard_map/ppermute | solution.py:15
  262.0 14.6 %collective-permute-start.17 = (f32[5,1,32,1440]{3,2,0,1:T(8,128)S(1)}, f32[5,1,32,1440]{3,2,0,1:T(8,128)S(1)}, u32[]{:S(2)}, u32[]{:S(2)}) collective-permute-start(f32[5,1,32,1440]{3,2,0,1:T(8,128)S(1)} %broadcast_select_fusion.5), channel_id=1, source_target_pairs={{0,4},{4,8},{8,12},{12,16},{16,20},{20,24},{24,28},{28,0},{1,5},{5... | collective-permute-start | bytes 2764808 | tf_op jit(solution)/shard_map/ppermute | solution.py:15
  285.4 20.3 %all-to-all-start.1 = ((f32[8,20,1440]{2,1,0:T(8,128)}), f32[8,20,1440]{2,1,0:T(8,128)S(1)}, u32[]{:S(2)}, u32[]{:S(2)}) async-start(f32[8,20,1440]{2,1,0:T(8,128)} %all_to_all.37), calls=%async_computation.1 | async-start | bytes 2359296 | tf_op jit(solution)/shard_map/all_to_all | solution.py:152
  332.5 6.7 %collective-permute-start.19 = (f32[20,1440]{1,0:T(8,128)S(1)}, f32[20,1440]{1,0:T(8,128)S(1)}, u32[]{:S(2)}, u32[]{:S(2)}) collective-permute-start(f32[20,1440]{1,0:T(8,128)S(1)} %get-tuple-element.28), channel_id=1, source_target_pairs={{0,8},{4,12},{8,0},{12,4},{16,24},{20,28},{24,16},{28,20},{1,9},{5... | collective-permute-start | bytes 345608 | tf_op jit(solution)/shard_map/ppermute | solution.py:165
  333.0 9.8 %collective-permute-start.20 = (f32[20,1440]{1,0:T(8,128)S(1)}, f32[20,1440]{1,0:T(8,128)S(1)}, u32[]{:S(2)}, u32[]{:S(2)}) collective-permute-start(f32[20,1440]{1,0:T(8,128)S(1)} %get-tuple-element.27), channel_id=1, source_target_pairs={{0,12},{4,8},{8,4},{12,0},{16,28},{20,24},{24,20},{28,16},{1,13},{... | collective-permute-start | bytes 345608 | tf_op jit(solution)/shard_map/ppermute | solution.py:165
  334.3 9.8 %collective-permute-start.21 = (f32[20,1440]{1,0:T(8,128)S(1)}, f32[20,1440]{1,0:T(8,128)S(1)}, u32[]{:S(2)}, u32[]{:S(2)}) collective-permute-start(f32[20,1440]{1,0:T(8,128)S(1)} %get-tuple-element.26), channel_id=1, source_target_pairs={{0,16},{4,20},{8,24},{12,28},{16,0},{20,4},{24,8},{28,12},{1,17},{... | collective-permute-start | bytes 345608 | tf_op jit(solution)/shard_map/ppermute | solution.py:165
  334.9 14.5 %collective-permute-start.22 = (f32[20,1440]{1,0:T(8,128)S(1)}, f32[20,1440]{1,0:T(8,128)S(1)}, u32[]{:S(2)}, u32[]{:S(2)}) collective-permute-start(f32[20,1440]{1,0:T(8,128)S(1)} %get-tuple-element.25), channel_id=1, source_target_pairs={{0,20},{4,16},{8,28},{12,24},{16,4},{20,0},{24,12},{28,8},{1,21},{... | collective-permute-start | bytes 345608 | tf_op jit(solution)/shard_map/ppermute | solution.py:165
  336.0 14.4 %collective-permute-start.23 = (f32[20,1440]{1,0:T(8,128)S(1)}, f32[20,1440]{1,0:T(8,128)S(1)}, u32[]{:S(2)}, u32[]{:S(2)}) collective-permute-start(f32[20,1440]{1,0:T(8,128)S(1)} %get-tuple-element.24), channel_id=1, source_target_pairs={{0,24},{4,28},{8,16},{12,20},{16,8},{20,12},{24,0},{28,4},{1,25},{... | collective-permute-start | bytes 345608 | tf_op jit(solution)/shard_map/ppermute | solution.py:165
  339.2 12.3 %collective-permute-start.24 = (f32[20,1440]{1,0:T(8,128)S(1)}, f32[20,1440]{1,0:T(8,128)S(1)}, u32[]{:S(2)}, u32[]{:S(2)}) collective-permute-start(f32[20,1440]{1,0:T(8,128)S(1)} %get-tuple-element.23), channel_id=1, source_target_pairs={{0,28},{4,24},{8,20},{12,16},{16,12},{20,8},{24,4},{28,0},{1,29},{... | collective-permute-start | bytes 345608 | tf_op jit(solution)/shard_map/ppermute | solution.py:165
  (7 other events, 69.1 us)
